TPU v7x, 32 devices: a whole 2x2x4 slice. The times are simulated.
32 devices in a mesh: expert: 8 (over z, x), tensor: 4 (over y, core).
Axes of the slice: x: 2, y: 2, z: 4, core: 2. Of those that a mesh axis runs over, the one named last changes fastest.
Arguments:
- tokens: bfloat16 [1024, 4096], P('expert', 'tensor'), may hold values from -6 to 6
- expert_ids: int32 [1024, 8], P('expert'), may hold values from 0 to 15, all different within a row; in each aligned block of 128 rows (0 to 127, 128 to 255, ...) at most 96 rows name the same one
- combine_weight: float32 [1024, 8], P('expert'), may hold values from 0.05 to 0.5
- gate_weight: bfloat16 [16, 4096, 1024], P('expert', 'tensor'), may hold values from -0.09375 to 0.09375
- up_weight: bfloat16 [16, 4096, 1024], P('expert', 'tensor'), may hold values from -0.09375 to 0.09375
- down_weight: bfloat16 [16, 1024, 4096], P('expert', None, 'tensor'), may hold values from -0.1875 to 0.1875
- out_cotangent: bfloat16 [1024, 4096], P('expert', 'tensor'), may hold values from -3 to 3
Outputs:
- mixed: bfloat16 [1024, 4096], P('expert', 'tensor')
- token_grad: bfloat16 [1024, 4096], P('expert', 'tensor')
- combine_grad: float32 [1024, 8], P('expert')
- gate_grad: bfloat16 [16, 4096, 1024], P('expert', 'tensor')
- up_grad: bfloat16 [16, 4096, 1024], P('expert', 'tensor')
- down_grad: bfloat16 [16, 1024, 4096], P('expert', None, 'tensor')
Inputs may be any that keep to these rules, and one draw needn't show every extreme that they name: `expert_ids`: each row names 8 different experts. Among the rows of one device no expert is named by more than 96 rows, a bound that some block reaches.
All inputs are finite; a program needn't handle non-finite values.
Results may differ from a plain program's by a relative error of at most 0.023.
Values may be sent and summed in bfloat16 or wider, within the bound.
A program may use at most 128 MiB of HBM per device.

v0:
```python
import jax
import jax.numpy as jnp
from jax import lax
from jax.sharding import PartitionSpec as P


def per_device(
    tokens, expert_ids, combine_weight, gate_weight, up_weight, down_weight, out_cotangent
):
    groups = lax.axis_size("expert")
    local_experts = gate_weight.shape[0]
    width_share = tokens.shape[1]
    hidden = gate_weight.shape[2]
    tok_rows = tokens.shape[0]
    top_count = expert_ids.shape[1]
    experts_all = local_experts * groups
    capacity = 3 * tok_rows * top_count // (2 * experts_all)
    pair_count = tok_rows * top_count
    slot_total = local_experts * groups * capacity
    share_rows = hidden // lax.axis_size("tensor")
    flat_ids = expert_ids.reshape(pair_count)
    onehot = (flat_ids[:, None] == jnp.arange(experts_all, dtype=jnp.int32)[None, :]).astype(
        jnp.int32
    )
    running = jnp.cumsum(onehot, axis=0)
    position = jnp.sum(running * onehot, axis=1) - 1
    slot_of_pair = flat_ids * capacity + position
    slot_pair = (
        jnp.full((experts_all * capacity,), pair_count, jnp.int32)
        .at[slot_of_pair]
        .set(jnp.arange(pair_count, dtype=jnp.int32))
    )
    filled = slot_pair < pair_count
    safe_pair = jnp.minimum(slot_pair, pair_count - 1)
    slot_token = safe_pair // top_count
    token_send = jnp.where(filled[:, None], tokens[slot_token], jnp.zeros((), jnp.bfloat16))
    token_send = token_send.reshape(groups, local_experts * capacity, width_share)
    slot_weight = jnp.where(filled, combine_weight.reshape(pair_count)[safe_pair], jnp.float32(0.0))
    grads_send = (slot_weight[:, None] * out_cotangent[slot_token].astype(jnp.float32)).astype(
        jnp.bfloat16
    )
    grads_send = grads_send.reshape(groups, local_experts * capacity, width_share)
    routed_raw = lax.all_to_all(token_send, "expert", split_axis=0, concat_axis=0, tiled=True)
    routed = routed_raw.reshape(groups, local_experts, capacity, width_share)
    gate_part = jnp.einsum(
        "secd,edk->kesc", routed, gate_weight, preferred_element_type=jnp.float32
    ).reshape(hidden, slot_total)
    up_part = jnp.einsum(
        "secd,edk->kesc", routed, up_weight, preferred_element_type=jnp.float32
    ).reshape(hidden, slot_total)
    totals = lax.psum(
        jnp.concatenate([gate_part, up_part], axis=1).astype(jnp.bfloat16), "tensor"
    ).astype(jnp.float32)
    gate_full = totals[:, :slot_total].reshape(hidden, local_experts, groups, capacity)
    up_full = totals[:, slot_total:].reshape(hidden, local_experts, groups, capacity)
    hidden_all = (jax.nn.silu(gate_full) * up_full).astype(jnp.bfloat16)
    own_rows = lax.dynamic_slice_in_dim(
        totals, lax.axis_index("tensor") * share_rows, share_rows, 0
    )
    gate_own = own_rows[:, :slot_total].reshape(share_rows, local_experts, groups, capacity)
    up_own = own_rows[:, slot_total:].reshape(share_rows, local_experts, groups, capacity)
    expert_out = jnp.einsum(
        "fesc,efd->secd", hidden_all, down_weight, preferred_element_type=jnp.float32
    ).astype(jnp.bfloat16)
    expert_out = expert_out.reshape(groups, local_experts * capacity, width_share)
    returned = lax.all_to_all(
        expert_out, "expert", split_axis=0, concat_axis=0, tiled=True
    ).reshape(experts_all * capacity, width_share)
    pair_out = returned[slot_of_pair].reshape(tok_rows, top_count, width_share).astype(jnp.float32)
    mixed = jnp.sum(pair_out * combine_weight[:, :, None], axis=1).astype(jnp.bfloat16)
    partial_dots = jnp.sum(pair_out * out_cotangent.astype(jnp.float32)[:, None, :], axis=2)
    combine_grad = lax.psum(partial_dots, "tensor")
    grads_raw = lax.all_to_all(grads_send, "expert", split_axis=0, concat_axis=0, tiled=True)
    incoming_gradient = grads_raw.reshape(groups, local_experts, capacity, width_share)
    hidden_state_cotangent = lax.psum_scatter(
        jnp.einsum(
            "secd,ekd->kesc", incoming_gradient, down_weight, preferred_element_type=jnp.float32
        )
        .reshape(lax.axis_size("tensor") * share_rows, slot_total)
        .astype(jnp.bfloat16),
        "tensor",
        scatter_dimension=0,
        tiled=True,
    ).astype(jnp.float32)
    hidden_state_cotangent = hidden_state_cotangent.reshape(
        share_rows, local_experts, groups, capacity
    )
    down_grad = jnp.einsum(
        "fesc,secd->efd", hidden_all, incoming_gradient, preferred_element_type=jnp.float32
    ).astype(jnp.bfloat16)
    sigma = jax.nn.sigmoid(gate_own)
    gate_diff = (hidden_state_cotangent * up_own * sigma * (1.0 + gate_own * (1.0 - sigma))).astype(
        jnp.bfloat16
    )
    up_diff = (hidden_state_cotangent * jax.nn.silu(gate_own)).astype(jnp.bfloat16)
    gate_diffs, up_diffs = (
        lax.all_gather(gate_diff, "tensor", axis=0, tiled=True),
        lax.all_gather(up_diff, "tensor", axis=0, tiled=True),
    )
    routed_grad = jnp.einsum(
        "fesc,edf->secd", gate_diffs, gate_weight, preferred_element_type=jnp.float32
    )
    routed_grad = routed_grad + jnp.einsum(
        "fesc,edf->secd", up_diffs, up_weight, preferred_element_type=jnp.float32
    )
    routed_grad = routed_grad.astype(jnp.bfloat16).reshape(
        groups, local_experts * capacity, width_share
    )
    grad_back = lax.all_to_all(
        routed_grad, "expert", split_axis=0, concat_axis=0, tiled=True
    ).reshape(experts_all * capacity, width_share)
    token_grad = jnp.sum(
        grad_back[slot_of_pair].reshape(tok_rows, top_count, width_share).astype(jnp.float32),
        axis=1,
    ).astype(jnp.bfloat16)
    gate_grad = jnp.einsum(
        "secd,fesc->edf", routed, gate_diffs, preferred_element_type=jnp.float32
    ).astype(jnp.bfloat16)
    up_grad = jnp.einsum(
        "secd,fesc->edf", routed, up_diffs, preferred_element_type=jnp.float32
    ).astype(jnp.bfloat16)
    return (mixed, token_grad, combine_grad, gate_grad, up_grad, down_grad)


def solution(mesh):
    placed = (
        P("expert", "tensor"),
        P("expert", None),
        P("expert", None),
        P("expert", "tensor", None),
        P("expert", "tensor", None),
        P("expert", None, "tensor"),
        P("expert", "tensor"),
    )
    return jax.shard_map(
        per_device,
        mesh=mesh,
        in_specs=placed,
        out_specs=(
            P("expert", "tensor"),
            P("expert", "tensor"),
            P("expert", None),
            P("expert", "tensor", None),
            P("expert", "tensor", None),
            P("expert", None, "tensor"),
        ),
        check_vma=False,
    )
```

profile of v0, /device:TPU:0, one launch (start us, length us, event | category | flops | bytes accessed | tf_op | source)
XLA Modules:
  0.0 478.2 jit_solution(15574865615111957846)
XLA Ops:
  19.3 5.9 %gather_fusion.2 = f32[1536]{0:T(1024)S(1)} fusion(f32[1024]{0:T(1024)S(1)} %reshape.156, s32[2048]{0:T(1024)S(1)} %get-tuple-element.22), kind=kCustom, calls=%fused_computation.2 | custom fusion | bytes 18432 | tf_op jit(solution)/shard_map/gather | solution.py:38
  25.3 5.1 %gather_fusion = bf16[1536,1024]{1,0:T(8,128)(2,1)S(1)} fusion(bf16[128,1024]{1,0:T(8,128)(2,1)S(1)} %copy-done, s32[2048]{0:T(1024)S(1)} %get-tuple-element.23), kind=kCustom, calls=%fused_computation | custom fusion | bytes 6297600 | tf_op jit(solution)/shard_map/gather | solution.py:36
  32.3 7.4 %all-to-all-start = ((bf16[8,192,1024]{2,1,0:T(8,128)(2,1)}), bf16[8,192,1024]{2,1,0:T(8,128)(2,1)}, u32[]{:S(2)}, u32[]{:S(2)}) async-start(bf16[8,192,1024]{2,1,0:T(8,128)(2,1)} %broadcast_select_fusion), calls=%async_computation | async-start | bytes 6291456 | tf_op jit(solution)/shard_map/all_to_all | solution.py:43
  47.1 63.4 %all-to-all-done = bf16[8,192,1024]{2,1,0:T(8,128)(2,1)} async-done(((bf16[8,192,1024]{2,1,0:T(8,128)(2,1)}), bf16[8,192,1024]{2,1,0:T(8,128)(2,1)}, u32[]{:S(2)}, u32[]{:S(2)}) %all-to-all-start) | async-done | bytes 3145760 | tf_op jit(solution)/shard_map/all_to_all | solution.py:43
  114.2 6.7 %fusion.34 = bf16[2,8,96,1024]{3,2,1,0:T(8,128)(2,1)S(1)} fusion(bf16[2,1024,1024]{2,1,0:T(8,128)(2,1)} %param.11, bf16[8,2,96,1024]{3,2,1,0:T(8,128)(2,1)} %bitcast.5), kind=kOutput, calls=%fused_computation.41 | convolution fusion | flops 3222798336 | bytes 10485760 | tf_op jit(solution)/shard_map/secd,edk->kesc/dot_general | solution.py:48
  120.9 5.5 %fusion.29 = bf16[2,8,96,1024]{3,2,1,0:T(8,128)(2,1)S(1)} fusion(bf16[2,1024,1024]{2,1,0:T(8,128)(2,1)S(1)} %copy-done.5, bf16[8,2,96,1024]{3,2,1,0:T(8,128)(2,1)} %bitcast.5), kind=kOutput, calls=%fused_computation.40 | convolution fusion | flops 3222798336 | bytes 10485760 | tf_op jit(solution)/shard_map/secd,edk->kesc/dot_general | solution.py:45
  129.9 55.1 %all-to-all-done.2 = bf16[8,192,1024]{2,1,0:T(8,128)(2,1)S(1)} async-done(((bf16[8,192,1024]{2,1,0:T(8,128)(2,1)}), bf16[8,192,1024]{2,1,0:T(8,128)(2,1)S(1)}, u32[]{:S(2)}, u32[]{:S(2)}) %all-to-all-start.2) | async-done | bytes 3145760 | tf_op jit(solution)/shard_map/all_to_all | solution.py:73
  185.0 8.2 %fusion.24 = bf16[2,8,96,1024]{3,2,1,0:T(8,128)(2,1)} fusion(bf16[2,1024,1024]{2,1,0:T(8,128)(2,1)} %param.12, bf16[8,2,96,1024]{3,2,1,0:T(8,128)(2,1)S(1)} %bitcast.103), kind=kOutput, calls=%fused_computation.39 | convolution fusion | flops 3222798336 | bytes 10485760 | tf_op jit(solution)/shard_map/secd,ekd->kesc/dot_general | solution.py:76
  193.7 57.2 %all-reduce.2.cloned.1.call-done = bf16[1024,3072]{0,1:T(8,128)(2,1)} async-done(((bf16[1024,3072]{0,1:T(8,128)(2,1)}), bf16[1024,3072]{0,1:T(8,128)(2,1)}) %all-reduce.2.cloned.1.call-update) | async-done | bytes 6291472 | tf_op jit(solution)/shard_map/psum | solution.py:51
  256.7 35.3 %reduce-scatter.2.cloned.1.call-done = bf16[256,1536]{0,1:T(8,128)(2,1)} async-done(((bf16[1024,1536]{0,1:T(8,128)(2,1)}), bf16[256,1536]{0,1:T(8,128)(2,1)}) %reduce-scatter.2.cloned.1.call-update) | async-done | bytes 786448 | tf_op jit(solution)/shard_map/reduce_scatter | solution.py:75
  301.7 7.1 %convert_bitcast_fusion = bf16[8,2,96,1024]{3,2,0,1:T(8,128)(2,1)S(1)} fusion(bf16[1024,2,8,96]{0,3,2,1:T(8,128)(2,1)S(1)} %multiply_convert_fusion, bf16[2,1024,1024]{2,1,0:T(8,128)(2,1)} %param.12), kind=kOutput, calls=%fused_computation.33 | convolution fusion | flops 3222798336 | bytes 10485760 | tf_op jit(solution)/shard_map/fesc,efd->secd/dot_general | solution.py:62
  310.8 5.8 %all-to-all-start.1 = ((bf16[8,192,1024]{2,1,0:T(8,128)(2,1)}), bf16[8,192,1024]{2,1,0:T(8,128)(2,1)S(1)}, u32[]{:S(2)}, u32[]{:S(2)}) async-start(bf16[8,192,1024]{2,1,0:T(8,128)(2,1)} %bitcast.98), calls=%async_computation.1 | async-start | bytes 6291456 | tf_op jit(solution)/shard_map/all_to_all | solution.py:66
  316.7 7.5 %all-gather.5.cloned.1.call-done = bf16[1024,2,8,96]{0,3,2,1:T(8,128)(2,1)} async-done(((bf16[256,2,8,96]{0,3,2,1:T(8,128)(2,1)}), bf16[1024,2,8,96]{0,3,2,1:T(8,128)(2,1)}) %all-gather.5.cloned.1.call-update) | async-done | bytes 3145744 | tf_op jit(solution)/shard_map/all_gather | solution.py:98
  324.2 9.4 %fusion.3 = f32[2,8,96,1024]{3,2,1,0:T(8,128)} fusion(bf16[1024,2,8,96]{0,3,2,1:T(8,128)(2,1)} %all-gather.5.cloned.1.call-done, bf16[2,1024,1024]{2,1,0:T(8,128)(2,1)} %param.11), kind=kOutput, calls=%fused_computation.18 | convolution fusion | flops 3221225472 | bytes 13631488 | tf_op jit(solution)/shard_map/fesc,edf->secd/dot_general | solution.py:103
  333.6 21.0 %all-gather.3.cloned.1.call-done = bf16[1024,2,8,96]{0,3,2,1:T(8,128)(2,1)} async-done(((bf16[256,2,8,96]{0,3,2,1:T(8,128)(2,1)}), bf16[1024,2,8,96]{0,3,2,1:T(8,128)(2,1)}) %all-gather.3.cloned.1.call-update) | async-done | bytes 3145744 | tf_op jit(solution)/shard_map/all_gather | solution.py:97
  354.6 8.4 %fusion.15 = bf16[8,2,96,1024]{3,2,0,1:T(8,128)(2,1)S(1)} fusion(f32[2,8,96,1024]{3,2,1,0:T(8,128)} %fusion.3, bf16[1024,2,8,96]{0,3,2,1:T(8,128)(2,1)} %all-gather.3.cloned.1.call-done, bf16[2,1024,1024]{2,1,0:T(8,128)(2,1)} %param.10), kind=kOutput, calls=%fused_computation.30 | convolution fusion | flops 3224371200 | bytes 16777216 | tf_op jit(solution)/shard_map/fesc,edf->secd/dot_general | solution.py:100
  364.9 22.4 %all-to-all-done.1 = bf16[8,192,1024]{2,1,0:T(8,128)(2,1)S(1)} async-done(((bf16[8,192,1024]{2,1,0:T(8,128)(2,1)}), bf16[8,192,1024]{2,1,0:T(8,128)(2,1)S(1)}, u32[]{:S(2)}, u32[]{:S(2)}) %all-to-all-start.1) | async-done | bytes 3145760 | tf_op jit(solution)/shard_map/all_to_all | solution.py:66
  392.6 8.3 %bitcast_convert_fusion = bf16[2,1024,1024]{2,1,0:T(8,128)(2,1)} fusion(bf16[1024,2,8,96]{0,3,2,1:T(8,128)(2,1)} %copy-done.4, bf16[8,2,96,1024]{3,2,1,0:T(8,128)(2,1)} %bitcast.104), kind=kOutput, calls=%fused_computation.6 | convolution fusion | flops 3223322624 | bytes 10485760 | tf_op jit(solution)/shard_map/fesc,secd->efd/dot_general | solution.py:88
  400.9 5.3 %gather_fusion.1 = bf16[1024,1024]{1,0:T(8,128)(2,1)} fusion(bf16[1536,1024]{1,0:T(8,128)(2,1)S(1)} %bitcast.94, s32[1024]{0:T(1024)S(1)} %broadcast_clamp_fusion), kind=kCustom, calls=%fused_computation.1 | custom fusion | bytes 4198400 | tf_op jit(solution)/shard_map/gather | solution.py:69
  410.5 11.7 %psum.15 = f32[128,8]{1,0:T(8,128)S(1)} all-reduce(f32[128,8]{1,0:T(8,128)S(1)} %get-tuple-element.12), channel_id=1, replica_groups=mesh['expert'=8,'tensor'=4] {'tensor'}, use_global_device_ids=true, to_apply=%region_9.10 | all-reduce | flops 1024 | bytes 8192 | tf_op jit(solution)/shard_map/psum | solution.py:72
  422.8 7.0 %bitcast_convert_fusion.1 = bf16[2,1024,1024]{2,1,0:T(8,128)(2,1)} fusion(bf16[8,2,96,1024]{3,2,1,0:T(8,128)(2,1)} %bitcast.5, bf16[1024,2,8,96]{0,3,2,1:T(8,128)(2,1)S(1)} %copy-done.6), kind=kOutput, calls=%fused_computation.7 | convolution fusion | flops 3223322624 | bytes 10485760 | tf_op jit(solution)/shard_map/secd,fesc->edf/dot_general | solution.py:119
  429.9 6.9 %bitcast_convert_fusion.2 = bf16[2,1024,1024]{2,1,0:T(8,128)(2,1)} fusion(bf16[8,2,96,1024]{3,2,1,0:T(8,128)(2,1)} %bitcast.5, bf16[1024,2,8,96]{0,3,2,1:T(8,128)(2,1)S(1)} %copy-done.7), kind=kOutput, calls=%fused_computation.8 | convolution fusion | flops 3223322624 | bytes 10485760 | tf_op jit(solution)/shard_map/secd,fesc->edf/dot_general | solution.py:116
  436.8 25.2 %all-to-all-done.3 = bf16[8,192,1024]{2,1,0:T(8,128)(2,1)} async-done(((bf16[8,192,1024]{2,1,0:T(8,128)(2,1)}), bf16[8,192,1024]{2,1,0:T(8,128)(2,1)}, u32[]{:S(2)}, u32[]{:S(2)}) %all-to-all-start.3) | async-done | bytes 3145760 | tf_op jit(solution)/shard_map/all_to_all | solution.py:109
  461.9 7.3 %gather_fusion.4 = bf16[1024,1024]{1,0:T(8,128)(2,1)S(1)} fusion(bf16[1536,1024]{1,0:T(8,128)(2,1)} %bitcast.35, s32[1024]{0:T(1024)S(1)} %broadcast_clamp_fusion), kind=kCustom, calls=%fused_computation.4 | custom fusion | bytes 4198400 | tf_op jit(solution)/shard_map/gather | solution.py:113
  (69 shorter events, 60.8 us)
Async XLA Ops:
  7.2 18.1 %copy-start = (bf16[128,1024]{1,0:T(8,128)(2,1)S(1)}, bf16[128,1024]{1,0:T(8,128)(2,1)}, u32[]{:S(2)}) copy-start(bf16[128,1024]{1,0:T(8,128)(2,1)} %param.7) | copy-start | bytes 786436
  32.3 7.5 %copy-start.2 = (bf16[128,1024]{1,0:T(8,128)(2,1)S(1)}, bf16[128,1024]{1,0:T(8,128)(2,1)}, u32[]{:S(2)}) copy-start(bf16[128,1024]{1,0:T(8,128)(2,1)} %param.13) | copy-start | bytes 786436
  32.3 78.2 %all-to-all-start = ((bf16[8,192,1024]{2,1,0:T(8,128)(2,1)}), bf16[8,192,1024]{2,1,0:T(8,128)(2,1)}, u32[]{:S(2)}, u32[]{:S(2)}) async-start(bf16[8,192,1024]{2,1,0:T(8,128)(2,1)} %broadcast_select_fusion), calls=%async_computation | async-start | bytes 6291456 | tf_op jit(solution)/shard_map/all_to_all | solution.py:43
  110.5 74.5 %all-to-all-start.2 = ((bf16[8,192,1024]{2,1,0:T(8,128)(2,1)}), bf16[8,192,1024]{2,1,0:T(8,128)(2,1)S(1)}, u32[]{:S(2)}, u32[]{:S(2)}) async-start(bf16[8,192,1024]{2,1,0:T(8,128)(2,1)} %fusion), calls=%async_computation.2 | async-start | bytes 6291456 | tf_op jit(solution)/shard_map/all_to_all | solution.py:73
  114.1 136.8 %all-reduce.2.cloned.1.call-start = ((), (), s32[]{:S(2)}) async-start(), calls=%async_computation.5 | async-start | bytes 12582912 | tf_op jit(solution)/shard_map/psum | solution.py:51
  114.2 6.7 %copy-start.5 = (bf16[2,1024,1024]{2,1,0:T(8,128)(2,1)S(1)}, bf16[2,1024,1024]{2,1,0:T(8,128)(2,1)}, u32[]{:S(2)}) copy-start(bf16[2,1024,1024]{2,1,0:T(8,128)(2,1)} %param.10) | copy-start | bytes 12582916
  129.8 162.2 %reduce-scatter.2.cloned.1.call-start = ((), (), s32[]{:S(2)}) async-start(), calls=%async_computation.6 | async-start | bytes 3932160 | tf_op jit(solution)/shard_map/reduce_scatter | solution.py:75
  185.0 8.2 %copy-start.3 = (bf16[8,192,1024]{2,1,0:T(8,128)(2,1)}, bf16[8,192,1024]{2,1,0:T(8,128)(2,1)S(1)}, u32[]{:S(2)}) copy-start(bf16[8,192,1024]{2,1,0:T(8,128)(2,1)S(1)} %all-to-all-done.2) | copy-start | bytes 9437188
  193.2 131.0 %all-gather.5.cloned.1.call-start = ((), (), s32[]{:S(2)}) async-start(), calls=%async_computation.8 | async-start | bytes 3932160 | tf_op jit(solution)/shard_map/all_gather | solution.py:98
  295.1 59.4 %all-gather.3.cloned.1.call-start = ((), (), s32[]{:S(2)}) async-start(), calls=%async_computation.7 | async-start | bytes 3932160 | tf_op jit(solution)/shard_map/all_gather | solution.py:97
  301.7 7.1 %copy-start.4 = (bf16[1024,2,8,96]{0,3,2,1:T(8,128)(2,1)}, bf16[1024,2,8,96]{0,3,2,1:T(8,128)(2,1)S(1)}, u32[]{:S(2)}) copy-start(bf16[1024,2,8,96]{0,3,2,1:T(8,128)(2,1)S(1)} %multiply_convert_fusion) | copy-start | bytes 9437188
  310.8 76.5 %all-to-all-start.1 = ((bf16[8,192,1024]{2,1,0:T(8,128)(2,1)}), bf16[8,192,1024]{2,1,0:T(8,128)(2,1)S(1)}, u32[]{:S(2)}, u32[]{:S(2)}) async-start(bf16[8,192,1024]{2,1,0:T(8,128)(2,1)} %bitcast.98), calls=%async_computation.1 | async-start | bytes 6291456 | tf_op jit(solution)/shard_map/all_to_all | solution.py:66
  387.3 74.7 %all-to-all-start.3 = ((bf16[8,192,1024]{2,1,0:T(8,128)(2,1)}), bf16[8,192,1024]{2,1,0:T(8,128)(2,1)}, u32[]{:S(2)}, u32[]{:S(2)}) async-start(bf16[8,192,1024]{2,1,0:T(8,128)(2,1)} %bitcast.97), calls=%async_computation.4 | async-start | bytes 6291456 | tf_op jit(solution)/shard_map/all_to_all | solution.py:109
  406.2 16.6 %copy-start.6 = (bf16[1024,2,8,96]{0,3,2,1:T(8,128)(2,1)S(1)}, bf16[1024,2,8,96]{0,3,2,1:T(8,128)(2,1)}, u32[]{:S(2)}) copy-start(bf16[1024,2,8,96]{0,3,2,1:T(8,128)(2,1)} %all-gather.5.cloned.1.call-done) | copy-start | bytes 9437188
  422.8 7.1 %copy-start.7 = (bf16[1024,2,8,96]{0,3,2,1:T(8,128)(2,1)S(1)}, bf16[1024,2,8,96]{0,3,2,1:T(8,128)(2,1)}, u32[]{:S(2)}) copy-start(bf16[1024,2,8,96]{0,3,2,1:T(8,128)(2,1)} %all-gather.3.cloned.1.call-done) | copy-start | bytes 9437188
  461.9 9.4 %copy-start.1 = (bf16[128,1024]{1,0:T(8,128)(2,1)S(1)}, bf16[128,1024]{1,0:T(8,128)(2,1)}, u32[]{:S(2)}) copy-start(bf16[128,1024]{1,0:T(8,128)(2,1)} %param.7) | copy-start | bytes 786436
Sparse Core Ops, SparseCore 0:
  130.0 120.9 all-reduce.1
  254.0 37.9 reduce-scatter.1
  295.3 28.9 all-gather.4
  325.6 28.8 all-gather.2
where the time goes:
time: 487 us; the launch traced here: 478 us
  waiting for transfers between devices  287 us (59%)
  matrix products  67.5 us (14%)
  local copies, waits for them, and re-layouts  46 us (9%)
  other arithmetic  29.6 us (6%)
  starting transfers between devices  22 us (5%)
  between operations  14.3 us (3%)
  blocking collectives  11.7 us (2%)
    all_to_all x1, waiting for transfers between devices, per_device(): lax.all_to_all(token_send, 'expert', split_axis=0, concat_axis=0, tiled=T...  63.4 us
    psum x1, waiting for transfers between devices, per_device(): lax.psum(jnp.concatenate([gate_part, up_part], axis=1).astype(jnp.bfloat1...  57.2 us
    all_to_all x1, waiting for transfers between devices, per_device(): lax.all_to_all(grads_send, 'expert', split_axis=0, concat_axis=0, tiled=T...  55.1 us
    reduce_scatter x1, waiting for transfers between devices, per_device(): lax.psum_scatter(jnp.einsum('secd,ekd->kesc', incoming_gradient, down_wei...  35.3 us
    all_to_all x1, waiting for transfers between devices, per_device(): lax.all_to_all(routed_grad, 'expert', split_axis=0, concat_axis=0, tiled=...  25.2 us
    all_to_all x1, waiting for transfers between devices, per_device(): lax.all_to_all(expert_out, 'expert', split_axis=0, concat_axis=0, tiled=T...  22.4 us
    all_gather x1, waiting for transfers between devices, per_device(): lax.all_gather(gate_diff, 'tensor', axis=0, tiled=True)  21 us
    psum x1, blocking collectives, per_device(): combine_grad = lax.psum(partial_dots, 'tensor')  11.7 us
  transfers between devices with their start and end apart: 8, of which 8 were waited for; matrix products, arithmetic and copies ran while one was open for 22% of the time, Pallas kernels for 0%

commit v1 on v0

--- a/solution.py
+++ b/solution.py
@@ -2,6 +2,11 @@
 import jax.numpy as jnp
 from jax import lax
 from jax.sharding import PartitionSpec as P
+
+
+def gather_and_add(value, axis):
+    parts = lax.all_gather(value, axis)
+    return jnp.sum(parts, axis=0)
 
 
 def per_device(
@@ -48,7 +53,7 @@
     up_part = jnp.einsum(
         "secd,edk->kesc", routed, up_weight, preferred_element_type=jnp.float32
     ).reshape(hidden, slot_total)
-    totals = lax.psum(
+    totals = gather_and_add(
         jnp.concatenate([gate_part, up_part], axis=1).astype(jnp.bfloat16), "tensor"
     ).astype(jnp.float32)
     gate_full = totals[:, :slot_total].reshape(hidden, local_experts, groups, capacity)

time: 487 us -> 544 us (1.12)
  blocking collectives: 11.7 us -> 164 us
  waiting for transfers between devices: 287 us -> 151 us
  local copies, waits for them, and re-layouts: 46 us -> 75.2 us
  other arithmetic: 29.6 us -> 51.6 us
  matrix products: 67.5 us -> 57.7 us
    all_to_all x0 -> x2, blocking collectives: none -> 152 us  [the longest x1 78 us: per_device(): lax.all_to_all(token_send, 'expert', split_axis=0, concat_axis=0, tiled=T...]
    all_to_all x2 -> x0, waiting for transfers between devices: 119 us -> none  [the longest x1 63.4 us: per_device(): lax.all_to_all(token_send, 'expert', split_axis=0, concat_axis=0, tiled=T...]
    all_gather x0 -> x1, waiting for transfers between devices: none -> 57.4 us  [gather_and_add(): parts = lax.all_gather(value, axis)]
    psum x1 -> x0, waiting for transfers between devices: 57.2 us -> none  [per_device(): lax.psum(jnp.concatenate([gate_part, up_part], axis=1).astype(jnp.bfloat1...]
    reduce_scatter x1, waiting for transfers between devices: 35.3 us -> 13.9 us  [per_device(): lax.psum_scatter(jnp.einsum('secd,ekd->kesc', incoming_gradient, down_wei...]
    reduce_sum x0 -> x1, other arithmetic: none -> 18.5 us  [gather_and_add(): return jnp.sum(parts, axis=0)]
    all_to_all x1, waiting for transfers between devices: 22.4 us -> 40.5 us  [per_device(): lax.all_to_all(expert_out, 'expert', split_axis=0, concat_axis=0, tiled=T...]
    slice x1 -> x2, local copies, waits for them, and re-layouts: 4.38 us -> 16.1 us  [per_device(): totals[:, :slot_total].reshape(hidden, local_experts, groups, capacity)]
  transfers between devices with their start and end apart: 8 -> 6, of which waited for: 8 -> 5; matrix products, arithmetic and copies ran while one was open for 22% -> 23% of each run, Pallas kernels for 0% -> 0%
where the time goes in v1:
time: 544 us; the launch traced here: 535 us
  blocking collectives  164 us (30%)
  waiting for transfers between devices  151 us (28%)
  local copies, waits for them, and re-layouts  75.2 us (14%)
  matrix products  57.7 us (11%)
  other arithmetic  51.6 us (9%)
  starting transfers between devices  21.3 us (4%)
  between operations  14.4 us (3%)
    all_to_all x1, blocking collectives, per_device(): lax.all_to_all(token_send, 'expert', split_axis=0, concat_axis=0, tiled=T...  78 us
    all_to_all x1, blocking collectives, per_device(): lax.all_to_all(grads_send, 'expert', split_axis=0, concat_axis=0, tiled=T...  74.1 us
    all_gather x1, waiting for transfers between devices, gather_and_add(): parts = lax.all_gather(value, axis)  57.4 us
    all_to_all x1, waiting for transfers between devices, per_device(): lax.all_to_all(expert_out, 'expert', split_axis=0, concat_axis=0, tiled=T...  40.5 us
    all_to_all x1, waiting for transfers between devices, per_device(): lax.all_to_all(routed_grad, 'expert', split_axis=0, concat_axis=0, tiled=...  29 us
    reduce_sum x1, other arithmetic, gather_and_add(): return jnp.sum(parts, axis=0)  18.5 us
    slice x2, local copies, waits for them, and re-layouts, per_device(): totals[:, :slot_total].reshape(hidden, local_experts, groups, capacity)  16.1 us
    reduce_scatter x1, waiting for transfers between devices, per_device(): lax.psum_scatter(jnp.einsum('secd,ekd->kesc', incoming_gradient, down_wei...  13.9 us
  transfers between devices with their start and end apart: 6, of which 5 were waited for; matrix products, arithmetic and copies ran while one was open for 23% of the time, Pallas kernels for 0%

profile of v1, /device:TPU:0, one launch (start us, length us, event | category | flops | bytes accessed | tf_op | source)
XLA Modules:
  0.0 535.0 jit_solution(13478847694117924862)
XLA Ops:
  19.4 5.9 %gather_fusion.2 = f32[1536]{0:T(1024)S(1)} fusion(f32[1024]{0:T(1024)S(1)} %reshape.181, s32[2048]{0:T(1024)S(1)} %get-tuple-element.34), kind=kCustom, calls=%fused_computation.2 | custom fusion | bytes 18432 | tf_op jit(solution)/shard_map/gather | solution.py:43
  25.3 5.1 gather_fusion
  30.9 78.0 %all_to_all.20 = bf16[8,192,1024]{2,1,0:T(8,128)(2,1)S(1)} all-to-all(bf16[8,192,1024]{2,1,0:T(8,128)(2,1)S(1)} %broadcast_select_fusion), channel_id=1, replica_groups=mesh['expert'=8,'tensor'=4] {'expert'}, dimensions={0} | all-to-all | bytes 6291456 | tf_op jit(solution)/shard_map/all_to_all | solution.py:48
  116.9 8.2 %fusion.34 = bf16[2,8,96,1024]{3,2,1,0:T(8,128)(2,1)} fusion(bf16[2,1024,1024]{2,1,0:T(8,128)(2,1)} %param.11, bf16[8,2,96,1024]{3,2,1,0:T(8,128)(2,1)} %bitcast.104), kind=kOutput, calls=%fused_computation.41 | convolution fusion | flops 3222798336 | bytes 10485760 | tf_op jit(solution)/shard_map/secd,edk->kesc/dot_general | solution.py:53
  129.7 5.3 pad_maximum_fusion
  141.7 74.1 %all_to_all.21 = bf16[8,192,1024]{2,1,0:T(8,128)(2,1)S(1)} all-to-all(bf16[8,192,1024]{2,1,0:T(8,128)(2,1)S(1)} %fusion), channel_id=1, replica_groups=mesh['expert'=8,'tensor'=4] {'expert'}, dimensions={0} | all-to-all | bytes 6291456 | tf_op jit(solution)/shard_map/all_to_all | solution.py:78
  220.7 11.0 %all-gather.8.cloned.1.call-start = ((), (), s32[]{:S(2)}) async-start(), calls=%async_computation.8 | async-start | bytes 3932160 | tf_op jit(solution)/shard_map/all_gather | solution.py:103
  231.6 57.4 %all-gather.4.cloned.1.call-done = bf16[4,1024,3072]{2,1,0:T(8,128)(2,1)} async-done(((bf16[1,1024,3072]{2,1,0:T(8,128)(2,1)}), bf16[4,1024,3072]{2,1,0:T(8,128)(2,1)}) %all-gather.4.cloned.1.call-update) | async-done | bytes 25165840 | tf_op jit(solution)/shard_map/all_gather | solution.py:8
  289.1 18.5 %reduce_sum.52 = bf16[1024,3072]{1,0:T(8,128)(2,1)} reduce(bf16[4,1024,3072]{2,1,0:T(8,128)(2,1)} %all-gather.4.cloned.1.call-done, bf16[]{:T(256)} %constant.49.clone.1), dimensions={0}, to_apply=%region_4.5 | reduce | flops 9437184 | bytes 31457282 | tf_op jit(solution)/shard_map/reduce_sum | solution.py:9
  316.1 13.9 %reduce-scatter.2.cloned.1.call-done = bf16[256,1536]{0,1:T(8,128)(2,1)} async-done(((bf16[1024,1536]{0,1:T(8,128)(2,1)}), bf16[256,1536]{0,1:T(8,128)(2,1)}) %reduce-scatter.2.cloned.1.call-update) | async-done | bytes 786448 | tf_op jit(solution)/shard_map/reduce_scatter | solution.py:80
  333.6 9.6 %fusion.52 = (f32[1024,1536]{1,0:T(8,128)}, f32[1024,1536]{1,0:T(8,128)}) fusion(bf16[1024,3072]{1,0:T(8,128)(2,1)} %reduce_sum.52), kind=kLoop, calls=%fused_computation.77 | loop fusion | bytes 25165824 | tf_op jit(solution)/shard_map/slice | solution.py:59
  343.1 6.6 %copy.81 = f32[1024,1536]{0,1:T(8,128)} copy(f32[1024,1536]{1,0:T(8,128)} %get-tuple-element.28) | data formatting | bytes 12582912 | tf_op jit(solution)/shard_map/slice | solution.py:59
  349.7 6.6 %copy.82 = f32[1024,1536]{0,1:T(8,128)} copy(f32[1024,1536]{1,0:T(8,128)} %get-tuple-element.29) | data formatting | bytes 12582912 | tf_op jit(solution)/shard_map/slice | solution.py:60
  356.4 5.8 %multiply_convert_fusion = bf16[1024,2,8,96]{0,3,2,1:T(8,128)(2,1)S(1)} fusion(f32[1024,2,8,96]{0,3,2,1:T(8,128)} %bitcast.96, f32[1024,2,8,96]{0,3,2,1:T(8,128)} %bitcast.95), kind=kLoop, calls=%fused_computation.13 | loop fusion | flops 9437184 | bytes 15728640 | tf_op jit(solution)/shard_map/convert_element_type | solution.py:61
  368.0 5.5 %all-to-all-start.1 = ((bf16[8,192,1024]{2,1,0:T(8,128)(2,1)}), bf16[8,192,1024]{2,1,0:T(8,128)(2,1)S(1)}, u32[]{:S(2)}, u32[]{:S(2)}) async-start(bf16[8,192,1024]{2,1,0:T(8,128)(2,1)} %bitcast.98), calls=%async_computation.1 | async-start | bytes 6291456 | tf_op jit(solution)/shard_map/all_to_all | solution.py:71
  373.5 9.4 %fusion.3 = f32[2,8,96,1024]{3,2,1,0:T(8,128)} fusion(bf16[1024,2,8,96]{0,3,2,1:T(8,128)(2,1)} %all-gather.8.cloned.1.call-done, bf16[2,1024,1024]{2,1,0:T(8,128)(2,1)} %param.11), kind=kOutput, calls=%fused_computation.18 | convolution fusion | flops 3221225472 | bytes 13631488 | tf_op jit(solution)/shard_map/fesc,edf->secd/dot_general | solution.py:108
  382.8 10.1 %all-gather.6.cloned.1.call-done = bf16[1024,2,8,96]{0,3,2,1:T(8,128)(2,1)} async-done(((bf16[256,2,8,96]{0,3,2,1:T(8,128)(2,1)}), bf16[1024,2,8,96]{0,3,2,1:T(8,128)(2,1)}) %all-gather.6.cloned.1.call-update) | async-done | bytes 3145744 | tf_op jit(solution)/shard_map/all_gather | solution.py:102
  392.9 8.4 %fusion.15 = bf16[8,2,96,1024]{3,2,0,1:T(8,128)(2,1)S(1)} fusion(f32[2,8,96,1024]{3,2,1,0:T(8,128)} %fusion.3, bf16[1024,2,8,96]{0,3,2,1:T(8,128)(2,1)} %all-gather.6.cloned.1.call-done, bf16[2,1024,1024]{2,1,0:T(8,128)(2,1)} %param.10), kind=kOutput, calls=%fused_computation.30 | convolution fusion | flops 3224371200 | bytes 16777216 | tf_op jit(solution)/shard_map/fesc,edf->secd/dot_general | solution.py:105
  403.4 40.5 %all-to-all-done.1 = bf16[8,192,1024]{2,1,0:T(8,128)(2,1)S(1)} async-done(((bf16[8,192,1024]{2,1,0:T(8,128)(2,1)}), bf16[8,192,1024]{2,1,0:T(8,128)(2,1)S(1)}, u32[]{:S(2)}, u32[]{:S(2)}) %all-to-all-start.1) | async-done | bytes 3145760 | tf_op jit(solution)/shard_map/all_to_all | solution.py:71
  449.4 8.5 %bitcast_convert_fusion = bf16[2,1024,1024]{2,1,0:T(8,128)(2,1)} fusion(bf16[1024,2,8,96]{0,3,2,1:T(8,128)(2,1)} %copy-done.6, bf16[8,2,96,1024]{3,2,1,0:T(8,128)(2,1)} %bitcast.108), kind=kOutput, calls=%fused_computation.6 | convolution fusion | flops 3223322624 | bytes 10485760 | tf_op jit(solution)/shard_map/fesc,secd->efd/dot_general | solution.py:93
  467.9 5.3 gather_fusion.1
  477.3 11.6 %psum.7 = f32[128,8]{1,0:T(8,128)S(1)} all-reduce(f32[128,8]{1,0:T(8,128)S(1)} %get-tuple-element.24), channel_id=1, replica_groups=mesh['expert'=8,'tensor'=4] {'tensor'}, use_global_device_ids=true, to_apply=%region_9.10 | all-reduce | flops 1024 | bytes 8192 | tf_op jit(solution)/shard_map/psum | solution.py:77
  489.6 29.0 %all-to-all-done.3 = bf16[8,192,1024]{2,1,0:T(8,128)(2,1)} async-done(((bf16[8,192,1024]{2,1,0:T(8,128)(2,1)}), bf16[8,192,1024]{2,1,0:T(8,128)(2,1)}, u32[]{:S(2)}, u32[]{:S(2)}) %all-to-all-start.3) | async-done | bytes 3145760 | tf_op jit(solution)/shard_map/all_to_all | solution.py:114
  518.6 7.3 %gather_fusion.4 = bf16[1024,1024]{1,0:T(8,128)(2,1)S(1)} fusion(bf16[1536,1024]{1,0:T(8,128)(2,1)} %bitcast.35, s32[1024]{0:T(1024)S(1)} %broadcast_clamp_fusion), kind=kCustom, calls=%fused_computation.4 | custom fusion | bytes 4198400 | tf_op jit(solution)/shard_map/gather | solution.py:118
  (82 shorter events, 79.0 us)
Async XLA Ops:
  7.2 18.2 %copy-start = (bf16[128,1024]{1,0:T(8,128)(2,1)S(1)}, bf16[128,1024]{1,0:T(8,128)(2,1)}, u32[]{:S(2)}) copy-start(bf16[128,1024]{1,0:T(8,128)(2,1)} %param.7) | copy-start | bytes 786436
  7.2 281.9 %all-gather.4.cloned.1.call-start = ((), (), s32[]{:S(2)}) async-start(), calls=%async_computation.5 | async-start | bytes 31457280 | tf_op jit(solution)/shard_map/all_gather | solution.py:8
  30.9 78.1 %copy-start.9 = (bf16[2,1024,1024]{2,1,0:T(8,128)(2,1)S(1)}, bf16[2,1024,1024]{2,1,0:T(8,128)(2,1)}, u32[]{:S(2)}) copy-start(bf16[2,1024,1024]{2,1,0:T(8,128)(2,1)} %param.10) | copy-start | bytes 12582916
  108.9 4.8 copy-start.3
  135.1 0.9 copy-start.2
  135.1 194.8 %reduce-scatter.2.cloned.1.call-start = ((), (), s32[]{:S(2)}) async-start(), calls=%async_computation.6 | async-start | bytes 3932160 | tf_op jit(solution)/shard_map/reduce_scatter | solution.py:80
  141.7 74.2 %copy-start.7 = (bf16[2,1024,1024]{2,1,0:T(8,128)(2,1)S(1)}, bf16[2,1024,1024]{2,1,0:T(8,128)(2,1)}, u32[]{:S(2)}) copy-start(bf16[2,1024,1024]{2,1,0:T(8,128)(2,1)} %param.12) | copy-start | bytes 12582916
  215.8 4.8 copy-start.5
  220.7 152.8 %all-gather.8.cloned.1.call-start = ((), (), s32[]{:S(2)}) async-start(), calls=%async_computation.8 | async-start | bytes 3932160 | tf_op jit(solution)/shard_map/all_gather | solution.py:103
  333.5 59.4 %all-gather.6.cloned.1.call-start = ((), (), s32[]{:S(2)}) async-start(), calls=%async_computation.7 | async-start | bytes 3932160 | tf_op jit(solution)/shard_map/all_gather | solution.py:102
  356.4 5.9 %copy-start.8 = (bf16[2,1024,1024]{2,1,0:T(8,128)(2,1)S(1)}, bf16[2,1024,1024]{2,1,0:T(8,128)(2,1)}, u32[]{:S(2)}) copy-start(bf16[2,1024,1024]{2,1,0:T(8,128)(2,1)} %param.12) | copy-start | bytes 12582916
  362.3 3.6 copy-start.6
  368.0 75.9 %all-to-all-start.1 = ((bf16[8,192,1024]{2,1,0:T(8,128)(2,1)}), bf16[8,192,1024]{2,1,0:T(8,128)(2,1)S(1)}, u32[]{:S(2)}, u32[]{:S(2)}) async-start(bf16[8,192,1024]{2,1,0:T(8,128)(2,1)} %bitcast.98), calls=%async_computation.1 | async-start | bytes 6291456 | tf_op jit(solution)/shard_map/all_to_all | solution.py:71
  443.9 74.7 %all-to-all-start.3 = ((bf16[8,192,1024]{2,1,0:T(8,128)(2,1)}), bf16[8,192,1024]{2,1,0:T(8,128)(2,1)}, u32[]{:S(2)}, u32[]{:S(2)}) async-start(bf16[8,192,1024]{2,1,0:T(8,128)(2,1)} %bitcast.97), calls=%async_computation.4 | async-start | bytes 6291456 | tf_op jit(solution)/shard_map/all_to_all | solution.py:114
  449.4 8.5 %copy-start.4 = (bf16[8,192,1024]{2,1,0:T(8,128)(2,1)S(1)}, bf16[8,192,1024]{2,1,0:T(8,128)(2,1)}, u32[]{:S(2)}) copy-start(bf16[8,192,1024]{2,1,0:T(8,128)(2,1)} %copy-done.3) | copy-start | bytes 9437188
  449.4 8.5 %copy-start.10 = (bf16[1024,2,8,96]{0,3,2,1:T(8,128)(2,1)S(1)}, bf16[1024,2,8,96]{0,3,2,1:T(8,128)(2,1)}, u32[]{:S(2)}) copy-start(bf16[1024,2,8,96]{0,3,2,1:T(8,128)(2,1)} %all-gather.8.cloned.1.call-done) | copy-start | bytes 9437188
  457.9 5.0 copy-start.11
  518.6 9.4 %copy-start.1 = (bf16[128,1024]{1,0:T(8,128)(2,1)S(1)}, bf16[128,1024]{1,0:T(8,128)(2,1)}, u32[]{:S(2)}) copy-start(bf16[128,1024]{1,0:T(8,128)(2,1)} %param.7) | copy-start | bytes 786436
Sparse Core Ops, SparseCore 0:
  135.2 153.8 all-gather.3
  292.2 37.7 reduce-scatter.1
  333.6 28.8 all-gather.7
  364.0 28.8 all-gather.5
